TPU v7x, 32 devices: a whole 2x2x4 slice. The times are simulated.
32 devices in a mesh: tm: 4 (over z), dp: 8 (over y, x, core).
Axes of the slice: x: 2, y: 2, z: 4, core: 2. Of those that a mesh axis runs over, the one named last changes fastest.
Arguments:
- loaded: bfloat16 [8, 32, 8, 16, 128], P('dp', 'tm'), may hold values from -6 to 6
- frame_index: int32 [8, 32], P('dp', 'tm'), may hold values from 0 to 31, as said below
- out_grad: bfloat16 [8, 32, 8, 16, 128], P('dp', 'tm'), may hold values from -6 to 6
- kernel: bfloat16 [3, 3, 3, 128, 128], replicated, may hold values from -0.109375 to 0.109375
- conv_bias: float32 [128], replicated, may hold values from -3 to 3
Outputs:
- activated: bfloat16 [8, 32, 8, 16, 128], P('dp', 'tm')
- input_grad: bfloat16 [8, 32, 8, 16, 128], P('dp', 'tm')
- kernel_grad: float32 [3, 3, 3, 128, 128], replicated
- bias_grad: float32 [128], replicated
Inputs may be any that keep to these rules, and one draw needn't show every extreme that they name: Each clip's row of frame_index holds every frame number once. Loader row r lies on loader shard r // 8, frame f belongs to owner f // 8; at most 3 rows of one loader shard belong to one owner, and in every clip every loader shard sends exactly 3 rows to one owner.
All inputs are finite; a program needn't handle non-finite values.
Results may differ from a plain program's by a relative error of at most 0.005.
Values may be sent and summed in bfloat16 or wider, within the bound.
A program may use at most 64 MiB of HBM per device.

v0:
```python
import functools
import math

import jax
import jax.numpy as jnp
from jax import lax
from jax.experimental import pallas as pl
from jax.experimental.pallas import tpu as pltpu
from jax.sharding import PartitionSpec as P

CAP = 3
F32, BF16 = jnp.float32, jnp.bfloat16


def each(first, last, step):
    if last - first <= 4:
        for i in range(first, last):
            step(i)
    else:
        lax.fori_loop(first, last, lambda i, carry: (step(i), carry)[1], 0)


def kernel_body(
    dims, ids, loaded, og_hbm, w_hbm, bias,
    act, igrad, total, bgrad,
    og, w, wt, slots, rslots, frames, xc, xt, gc, dwf, dwb,
    pair_in, s32, s16, xy_in, z32, z16, z_in, b_own, b_pair, bx, bz,
    ld_sem, f_s, f_r, h_s, h_r, g_s, g_r, p_s, p_r, x_s, x_r, zs_s, zs_r,
    az_s, az_r, ax_s, ax_r, ap_s, ap_r, bp_s, bp_r, bx_s, bx_r, bz_s, bz_r,
):
    T, D, F, H, W, C, R, U = dims
    Q = D // 2
    HW = H * W
    K3 = 3 * C
    z = lax.axis_index("tm")
    dp = lax.axis_index("dp")
    c, q = dp % 2, dp // 2

    def at(tm=None, chip=None, core=None):
        return {
            "tm": z if tm is None else tm,
            "dp": (q if chip is None else chip) * 2 + (c if core is None else core),
        }

    def to_z(k):
        return at(tm=(z + k) % T)

    def to_q(k):
        return at(chip=(q + k) % Q)

    other = at(core=1 - c)

    def remote(src, dst, ss, rs, where):
        return pltpu.make_async_remote_copy(
            src_ref=src, dst_ref=dst, send_sem=ss, recv_sem=rs,
            device_id=where, device_id_type=pl.DeviceIdType.MESH,
        )

    load_w = pltpu.make_async_copy(w_hbm, w, ld_sem.at[0])
    load_og = pltpu.make_async_copy(og_hbm, og, ld_sem.at[1])
    load_w.start()
    load_og.start()

    barrier = pltpu.get_barrier_semaphore()

    def greet(where):
        pl.semaphore_signal(barrier, 1, device_id=where, device_id_type=pl.DeviceIdType.MESH)

    greet(other)
    each(1, Q, lambda k: greet(to_q(k)))
    each(1, T, lambda k: greet(to_z(k)))

    owners = [ids[0, r] // F for r in range(F)]
    rank = []
    for r in range(F):
        before = jnp.int32(0)
        for s in range(r):
            before = before + jnp.where(owners[s] == owners[r], 1, 0)
        rank.append(before)

    def pack(k):
        owner = (z + k) % T
        for s in range(CAP):
            row, target = jnp.int32(0), jnp.int32(-1)
            for r in range(F):
                hit = jnp.logical_and(owners[r] == owner, rank[r] == s)
                row = jnp.where(hit, r, row)
                target = jnp.where(hit, ids[0, r] - owner * F, target)
            slots[k, s, 0:H] = loaded[row]
            slots[k, s, H] = jnp.full((W, C), target.astype(F32), F32).astype(BF16)

    each(0, T, pack)
    pl.semaphore_wait(barrier, 1 + (Q - 1) + (T - 1))

    def row_copy(k):
        return remote(slots.at[k], rslots.at[k], f_s.at[k], f_r.at[k], to_z(k))

    each(1, T, lambda k: row_copy(k).start())

    for e in range(F + 2):
        for ref in (xc, gc):
            ref[e, 0] = jnp.zeros((W, K3), BF16)
            ref[e, H + 1] = jnp.zeros((W, K3), BF16)
    taps_rows = 3 * K3
    if D * R > taps_rows:
        for a in range(3):
            dwf[a, taps_rows:] = jnp.zeros((D * R - taps_rows, C), F32)
            dwb[a, taps_rows:] = jnp.zeros((D * R - taps_rows, C), BF16)
    if T * U > 3 * R:
        z32[3 * R :] = jnp.zeros((T * U - 3 * R, C), F32)
        z16[3 * R :] = jnp.zeros((T * U - 3 * R, C), BF16)
    load_w.wait()
    for p in range(9):
        for j in range(3):
            wt[p, j * C : (j + 1) * C, :] = w[p, j * C : (j + 1) * C, :].T
    load_og.wait()

    each(1, T, lambda k: row_copy(k).wait_recv())

    def place(f):
        picked = jnp.zeros((H, W, C), BF16)
        for k in range(T):
            source = slots if k == 0 else rslots
            for s in range(CAP):
                gap = jnp.abs(source[k, s, H] - jnp.asarray(f, BF16))
                weight = jnp.maximum(jnp.asarray(1, BF16) - gap, jnp.asarray(0, BF16))
                picked = picked + source[k, s, 0:H] * weight[None]
        frames[f + 2] = picked

    for f in (F - 2, F - 1):
        place(f)

    def halo_copy():
        return remote(frames.at[pl.ds(F, 2)], frames.at[pl.ds(0, 2)], h_s, h_r, to_z(1))

    def gate_copy():
        return remote(
            gate_out, gate_in, g_s, g_r, to_z(T - 1)
        )

    @pl.when(z < T - 1)
    def _():
        halo_copy().start()

    for f in range(F - 2):
        place(f)

    column = lax.broadcasted_iota(jnp.int32, (HW, C), 0) % W

    def shifted(value):
        left = jnp.where(column == 0, 0.0, pltpu.roll(value, 1, 0))
        right = jnp.where(column == W - 1, 0.0, pltpu.roll(value, HW - 1, 0))
        return left.astype(BF16), right.astype(BF16)

    def spread(e):
        mid = frames[e].reshape(HW, C)
        left, right = shifted(mid.astype(F32))
        for j, part in enumerate((left, mid, right)):
            xc[e, 1 : H + 1, :, j * C : (j + 1) * C] = part.reshape(H, W, C)
            xt[j * C : (j + 1) * C, e * HW : (e + 1) * HW] = part.T

    for e in range(2, F + 2):
        spread(e)

    def forward(t, n):
        pre = jnp.broadcast_to(bias[...], (n * HW, C))
        for a in range(3):
            for i in range(3):
                rows = xc[t + a : t + a + n, i : i + H].reshape(n * HW, K3)
                pre = pre + jnp.dot(rows, w[a * 3 + i], preferred_element_type=F32)
        sigma = jax.nn.sigmoid(pre)
        act[t : t + n] = (pre * sigma).astype(BF16).reshape(n, H, W, C)
        cot = og[t : t + n].reshape(n * HW, C).astype(F32)
        gate = (cot * sigma * (1.0 + pre * (1.0 - sigma))).astype(BF16)
        gc[t : t + n, 1 : H + 1, :, C : 2 * C] = gate.reshape(n, H, W, C)
        return jnp.sum(gate.astype(F32).reshape(n * HW // 8, 8, C), axis=0)

    bias_sum = jnp.zeros((8, C), F32)
    for t in range(2, F, 2):
        bias_sum = bias_sum + forward(t, 2)

    @pl.when(z > 0)
    def _():
        halo_copy().wait_recv()

    @pl.when(z == 0)
    def _():
        frames[0:2] = jnp.zeros((2, H, W, C), BF16)

    for e in range(2):
        spread(e)
    bias_sum = bias_sum + forward(0, 2)
    b_own[...] = bias_sum

    gate_out, gate_in = frames.at[pl.ds(F + 2, 2)], frames.at[pl.ds(F + 4, 2)]
    for t in range(2):
        frames[F + 2 + t] = gc[t, 1 : H + 1, :, C : 2 * C]

    @pl.when(z > 0)
    def _():
        gate_copy().start()

    half = Q * R

    def my_half(core):
        return pl.ds(pl.multiple_of(core * half, 16), half)

    def pair_copy(a):
        return remote(dwb.at[a, my_half(1 - c)], pair_in.at[a], p_s.at[a], p_r.at[a], other)

    def xy_copy(a, k):
        there = pl.ds(pl.multiple_of(((q + k) % Q) * R, 16), R)
        return remote(
            s16.at[a, there], xy_in.at[a, k], x_s.at[a, k], x_r.at[a, k], to_q(k)
        )

    def z_copy(k):
        there = pl.ds(pl.multiple_of(((z + k) % T) * U, 16), U)
        return remote(z16.at[there], z_in.at[k], zs_s.at[k], zs_r.at[k], to_z(k))

    def bias_pair():
        return remote(b_own, b_pair, bp_s, bp_r, other)

    def bias_q(k):
        return remote(bx.at[q], bx.at[q], bx_s.at[k], bx_r.at[k], to_q(k))

    def bias_z(k):
        return remote(bz.at[z], bz.at[z], bz_s.at[k], bz_r.at[k], to_z(k))

    def weight_term(a):
        gates = jnp.concatenate(
            [
                gc[0:F, 2 - i : 2 - i + H, :, C : 2 * C].reshape(F * HW, C)
                for i in range(3)
            ],
            axis=1,
        )
        term = jnp.dot(xt[:, a * HW : (a + F) * HW], gates, preferred_element_type=F32)
        for i in range(3):
            block = term[:, i * C : (i + 1) * C]
            dwf[a, i * K3 : (i + 1) * K3] = block
            dwb[a, i * K3 : (i + 1) * K3] = block.astype(BF16)

    def after_pair(a):
        pair_copy(a).wait_recv()
        both = dwf[a, my_half(c)] + pair_in[a].astype(F32)
        s32[a] = both
        s16[a] = both.astype(BF16)
        each(1, Q, lambda k: xy_copy(a, k).start())

    bias_pair().start()
    weight_term(0)
    pair_copy(0).start()
    weight_term(1)
    pair_copy(1).start()
    after_pair(0)
    weight_term(2)
    pair_copy(2).start()
    after_pair(1)
    bias_pair().wait_recv()
    bx[q] = b_own[...] + b_pair[...]
    each(1, Q, lambda k: bias_q(k).start())

    def spread_gate(t, mid):
        left, right = shifted(mid.astype(F32))
        gc[t, 1 : H + 1, :, 0:C] = right.reshape(H, W, C)
        gc[t, 1 : H + 1, :, 2 * C :] = left.reshape(H, W, C)

    for t in range(F):
        spread_gate(t, gc[t, 1 : H + 1, :, C : 2 * C].reshape(HW, C))
    after_pair(2)

    def backward(t, n):
        out = jnp.zeros((n * HW, C), F32)
        for a in range(3):
            for i in range(3):
                rows = gc[t + 2 - a : t + 2 - a + n, 2 - i : 2 - i + H].reshape(n * HW, K3)
                out = out + jnp.dot(rows, wt[a * 3 + i], preferred_element_type=F32)
        igrad[t : t + n] = out.astype(BF16).reshape(n, H, W, C)

    backward(0, 2)
    backward(2, 2)

    def after_xy(a):
        here = pl.ds(pl.multiple_of(q * R, 16), R)
        each(1, Q, lambda k: xy_copy(a, k).wait_recv())
        got = s32[a, here]
        for k in range(1, Q):
            got = got + xy_in[a, k].astype(F32)
        z32[a * R : (a + 1) * R] = got
        z16[a * R : (a + 1) * R] = got.astype(BF16)

    for a in range(3):
        after_xy(a)
    each(1, T, lambda k: z_copy(k).start())
    each(1, Q, lambda k: bias_q(k).wait_recv())
    got = bx[0]
    for k in range(1, Q):
        got = got + bx[k]
    bz[z] = got
    each(1, T, lambda k: bias_z(k).start())

    backward(4, 2)

    each(1, T, lambda k: z_copy(k).wait_recv())
    got = z32[pl.ds(pl.multiple_of(z * U, 16), U)]
    for k in range(1, T):
        got = got + z_in[k].astype(F32)
    block = c * Q + q
    total[block, z] = got.astype(BF16)

    def piece(k, kz):
        return total.at[c * Q + (q + Q - k) % Q, (z + T - kz) % T]

    def gather_z(k):
        return remote(piece(0, 0), piece(0, 0), az_s.at[k], az_r.at[k], to_z(k))

    def gather_q(kz, k):
        return remote(piece(0, kz), piece(0, kz), ax_s.at[kz, k], ax_r.at[kz, k], to_q(k))

    def gather_pair(kz, k):
        return remote(piece(k, kz), piece(k, kz), ap_s.at[kz, k], ap_r.at[kz, k], other)

    def send_on(kz):
        each(1, Q, lambda k: gather_q(kz, k).start())
        gather_pair(kz, 0).start()

    each(1, T, lambda k: gather_z(k).start())
    send_on(0)

    @pl.when(z < T - 1)
    def _():
        gate_copy().wait_recv()

    @pl.when(z == T - 1)
    def _():
        frames[F + 4 : F + 6] = jnp.zeros((2, H, W, C), BF16)

    for t in range(2):
        mid = frames[F + 4 + t]
        gc[F + t, 1 : H + 1, :, C : 2 * C] = mid
        spread_gate(F + t, mid.reshape(HW, C))

    def relay_z(kz):
        gather_z(kz).wait_recv()
        send_on(kz)

    def relay_q(kz):
        def one(k):
            gather_q(kz, k).wait_recv()
            gather_pair(kz, k).start()

        each(1, Q, one)

    each(1, T, relay_z)
    backward(6, 2)
    each(0, T, relay_q)

    each(1, T, lambda k: bias_z(k).wait_recv())
    got = bz[0]
    for k in range(1, T):
        got = got + bz[k]
    bgrad[...] = jnp.sum(got, axis=0, keepdims=True)

    each(0, T, lambda kz: each(0, Q, lambda k: gather_pair(kz, k).wait_recv()))

    each(1, T, lambda k: row_copy(k).wait_send())

    @pl.when(z < T - 1)
    def _():
        halo_copy().wait_send()

    @pl.when(z > 0)
    def _():
        gate_copy().wait_send()

    bias_pair().wait_send()
    each(1, Q, lambda k: bias_q(k).wait_send())
    each(1, T, lambda k: bias_z(k).wait_send())
    for a in range(3):
        pair_copy(a).wait_send()
        each(1, Q, lambda k: xy_copy(a, k).wait_send())
    each(1, T, lambda k: z_copy(k).wait_send())
    each(1, T, lambda k: gather_z(k).wait_send())
    each(0, T, lambda kz: each(1, Q, lambda k: gather_q(kz, k).wait_send()))
    each(0, T, lambda kz: each(0, Q, lambda k: gather_pair(kz, k).wait_send()))


def body(T, D, loaded, frame_index, out_grad, kernel, conv_bias):
    _, F, H, W, C = loaded.shape
    Q = D // 2
    K3, HW = 3 * C, H * W
    R = 16 * pl.cdiv(pl.cdiv(3 * K3, 16), D)
    U = 16 * pl.cdiv(3 * R // 16, T)
    dims = (T, D, F, H, W, C, R, U)
    vmem = pl.BlockSpec(memory_space=pltpu.VMEM)
    hbm = pl.BlockSpec(memory_space=pl.ANY)
    V = pltpu.VMEM
    S = pltpu.SemaphoreType.DMA
    act, igrad, total, bgrad = pl.pallas_call(
        functools.partial(kernel_body, dims),
        out_shape=(
            jax.ShapeDtypeStruct((F, H, W, C), BF16),
            jax.ShapeDtypeStruct((F, H, W, C), BF16),
            jax.ShapeDtypeStruct((D, T, U, C), BF16),
            jax.ShapeDtypeStruct((1, C), F32),
        ),
        in_specs=[pl.BlockSpec(memory_space=pltpu.SMEM), vmem, hbm, hbm, vmem],
        out_specs=(vmem, vmem, vmem, vmem),
        scratch_shapes=[
            V((F, H, W, C), BF16), V((9, K3, C), BF16), V((9, K3, C), BF16),
            V((T, CAP, H + 1, W, C), BF16), V((T, CAP, H + 1, W, C), BF16),
            V((F + 6, H, W, C), BF16),
            V((F + 2, H + 2, W, K3), BF16), V((K3, (F + 2) * HW), BF16),
            V((F + 2, H + 2, W, K3), BF16),
            V((3, D * R, C), F32), V((3, D * R, C), BF16),
            V((3, Q * R, C), BF16), V((3, Q * R, C), F32), V((3, Q * R, C), BF16),
            V((3, Q, R, C), BF16), V((T * U, C), F32), V((T * U, C), BF16),
            V((T, U, C), BF16),
            V((8, C), F32), V((8, C), F32), V((Q, 8, C), F32), V((T, 8, C), F32),
            S((2,)), S((T,)), S((T,)), S, S, S, S,
            S((3,)), S((3,)), S((3, Q)), S((3, Q)), S((T,)), S((T,)),
            S((T,)), S((T,)), S((T, Q)), S((T, Q)), S((T, Q)), S((T, Q)),
            S, S, S((Q,)), S((Q,)), S((T,)), S((T,)),
        ],
        compiler_params=pltpu.CompilerParams(
            collective_id=0, has_side_effects=True, vmem_limit_bytes=48 * 1024 * 1024
        ),
    )(frame_index, loaded[0], out_grad[0], kernel.reshape(9, K3, C), conv_bias[None])
    scale = 1.0 / math.sqrt(T * F * HW * D * loaded.shape[0])
    rows = total.reshape(D, T * U, C)[:, : 3 * R].reshape(D, 3, R, C)
    rows = jnp.swapaxes(rows, 0, 1).reshape(3, D * R, C)[:, : 3 * K3]
    kernel_grad = (rows.astype(F32) * scale).reshape(kernel.shape)
    return act[None], igrad[None], kernel_grad, bgrad[0] * scale


def solution(mesh):
    spread = P("dp", "tm", None, None, None)
    return jax.shard_map(
        functools.partial(body, mesh.shape["tm"], mesh.shape["dp"]),
        mesh=mesh,
        in_specs=(spread, P("dp", "tm"), spread, P(), P()),
        out_specs=(spread, spread, P(), P()),
        check_vma=False,
    )
```

profile of v0, /device:TPU:0, one launch (start us, length us, event | category | flops | bytes accessed | tf_op | source)
XLA Modules:
  0.0 52.9 jit_solution(5848900432757011709)
XLA Ops:
  0.6 0.0 copy-start
  0.6 1.2 %copy-done = bf16[3,3,3,128,128]{4,3,2,1,0:T(8,128)(2,1)S(1)} copy-done((bf16[3,3,3,128,128]{4,3,2,1,0:T(8,128)(2,1)S(1)}, bf16[3,3,3,128,128]{4,3,2,1,0:T(8,128)(2,1)}, u32[]{:S(2)}) %copy-start) | copy-done | bytes 884760
  1.8 0.0 copy-start.1
  1.8 0.9 %copy-done.1 = bf16[1,8,8,16,128]{4,3,2,1,0:T(8,128)(2,1)S(1)} copy-done((bf16[1,8,8,16,128]{4,3,2,1,0:T(8,128)(2,1)S(1)}, bf16[1,8,8,16,128]{4,3,2,1,0:T(8,128)(2,1)}, u32[]{:S(2)}) %copy-start.1) | copy-done | bytes 262168
  2.8 0.0 copy-start.2
  2.8 0.9 %copy-done.2 = bf16[1,8,8,16,128]{4,3,2,1,0:T(8,128)(2,1)S(1)} copy-done((bf16[1,8,8,16,128]{4,3,2,1,0:T(8,128)(2,1)S(1)}, bf16[1,8,8,16,128]{4,3,2,1,0:T(8,128)(2,1)}, u32[]{:S(2)}) %copy-start.2) | copy-done | bytes 262168
  3.7 0.0 copy-start.3
  3.7 0.7 %copy-done.3 = s32[1,8]{1,0:T(1,128)S(1)} copy-done((s32[1,8]{1,0:T(1,128)S(1)}, s32[1,8]{1,0:T(1,128)}, u32[]{:S(2)}) %copy-start.3) | copy-done | bytes 56
  4.4 0.0 copy-start.4
  4.4 0.7 %copy-done.4 = f32[128]{0:T(128)S(1)} copy-done((f32[128]{0:T(128)S(1)}, f32[128]{0:T(128)}, u32[]{:S(2)}) %copy-start.4) | copy-done | bytes 536
  5.0 44.5 %shard_map.84 = (bf16[8,8,16,128]{3,2,1,0:T(8,128)(2,1)S(1)}, bf16[8,8,16,128]{3,2,1,0:T(8,128)(2,1)S(1)}, bf16[8,4,112,128]{3,2,1,0:T(8,128)(2,1)S(1)}, f32[1,128]{1,0:T(1,128)S(1)}) custom-call(s32[1,8]{1,0:T(1,128)S(1)} %copy-done.3, bf16[8,8,16,128]{3,2,1,0:T(8,128)(2,1)S(1)} %bitcast.15, bf16[8,8,16,128]{3,2,1,0:T(8,128)(2,1)S(1)} %bitcast.16, ...), custom_call_target="tpu_custom_call" | custom-call | tf_op jit(solution)/shard_map/pallas_call | solution.py:400
  49.5 0.5 multiply_bitcast_fusion
  50.1 0.1 convert_multiply_fusion
  50.2 1.3 %copy.9 = f32[8,3,144,128]{3,2,0,1:T(8,128)} copy(f32[8,3,144,128]{3,2,1,0:T(8,128)S(1)} %bitcast.20) | data formatting | bytes 3538944 | tf_op jit(solution)/shard_map/mul | solution.py:433
  51.5 0.7 %copy.12 = bf16[1,8,8,16,128]{4,3,2,1,0:T(8,128)(2,1)} copy(bf16[1,8,8,16,128]{4,3,2,1,0:T(8,128)(2,1)S(1)} %bitcast.18) | data formatting | bytes 524288
  52.2 0.7 %copy.13 = bf16[1,8,8,16,128]{4,3,2,1,0:T(8,128)(2,1)} copy(bf16[1,8,8,16,128]{4,3,2,1,0:T(8,128)(2,1)S(1)} %bitcast.17) | data formatting | bytes 524288
Async XLA Ops:
  0.6 1.2 %copy-start = (bf16[3,3,3,128,128]{4,3,2,1,0:T(8,128)(2,1)S(1)}, bf16[3,3,3,128,128]{4,3,2,1,0:T(8,128)(2,1)}, u32[]{:S(2)}) copy-start(bf16[3,3,3,128,128]{4,3,2,1,0:T(8,128)(2,1)} %param.8) | copy-start | bytes 2654212
  1.8 0.9 %copy-start.1 = (bf16[1,8,8,16,128]{4,3,2,1,0:T(8,128)(2,1)S(1)}, bf16[1,8,8,16,128]{4,3,2,1,0:T(8,128)(2,1)}, u32[]{:S(2)}) copy-start(bf16[1,8,8,16,128]{4,3,2,1,0:T(8,128)(2,1)} %param.5) | copy-start | bytes 786436
  2.8 0.9 %copy-start.2 = (bf16[1,8,8,16,128]{4,3,2,1,0:T(8,128)(2,1)S(1)}, bf16[1,8,8,16,128]{4,3,2,1,0:T(8,128)(2,1)}, u32[]{:S(2)}) copy-start(bf16[1,8,8,16,128]{4,3,2,1,0:T(8,128)(2,1)} %param.7) | copy-start | bytes 786436
  3.7 0.7 %copy-start.3 = (s32[1,8]{1,0:T(1,128)S(1)}, s32[1,8]{1,0:T(1,128)}, u32[]{:S(2)}) copy-start(s32[1,8]{1,0:T(1,128)} %ids.1) | copy-start | bytes 100
  4.4 0.7 %copy-start.4 = (f32[128]{0:T(128)S(1)}, f32[128]{0:T(128)}, u32[]{:S(2)}) copy-start(f32[128]{0:T(128)} %param.9) | copy-start | bytes 1540
where the time goes:
time: 53.2 us; the launch traced here: 52.9 us
  Pallas kernels  44.5 us (84%)
  local copies, waits for them, and re-layouts  7.11 us (13%)
  between operations  0.66 us (1%)
  other arithmetic  0.65 us (1%)
    pallas_call x1, Pallas kernels, body(): pl.pallas_call(functools.partial(kernel_body, dims), out_shape=(jax.Shape...  44.5 us
    unnamed x12, local copies, waits for them, and re-layouts  5.77 us
    mul x1, local copies, waits for them, and re-layouts, body(): kernel_grad = (rows.astype(F32) * scale).reshape(kernel.shape)  1.34 us

commit v1 on v0

--- a/solution.py
+++ b/solution.py
@@ -21,9 +21,9 @@
 
 
 def kernel_body(
-    dims, ids, loaded, og_hbm, w_hbm, bias,
+    dims, ids_hbm, loaded_hbm, og_hbm, w_hbm, bias_hbm,
     act, igrad, total, bgrad,
-    og, w, wt, slots, rslots, frames, xc, xt, gc, dwf, dwb,
+    ids, loaded, bias, og, w, wt, slots, rslots, frames, xc, xt, gc, dwf, dwb,
     pair_in, s32, s16, xy_in, z32, z16, z_in, b_own, b_pair, bx, bz,
     ld_sem, f_s, f_r, h_s, h_r, g_s, g_r, p_s, p_r, x_s, x_r, zs_s, zs_r,
     az_s, az_r, ax_s, ax_r, ap_s, ap_r, bp_s, bp_r, bx_s, bx_r, bz_s, bz_r,
@@ -56,10 +56,14 @@
             device_id=where, device_id_type=pl.DeviceIdType.MESH,
         )
 
-    load_w = pltpu.make_async_copy(w_hbm, w, ld_sem.at[0])
-    load_og = pltpu.make_async_copy(og_hbm, og, ld_sem.at[1])
-    load_w.start()
-    load_og.start()
+    loads = [
+        pltpu.make_async_copy(source, target, ld_sem.at[n])
+        for n, (source, target) in enumerate(
+            [(ids_hbm, ids), (loaded_hbm, loaded), (w_hbm, w), (og_hbm, og), (bias_hbm, bias)]
+        )
+    ]
+    for load in loads:
+        load.start()
 
     barrier = pltpu.get_barrier_semaphore()
 
@@ -69,6 +73,9 @@
     greet(other)
     each(1, Q, lambda k: greet(to_q(k)))
     each(1, T, lambda k: greet(to_z(k)))
+
+    loads[0].wait()
+    loads[1].wait()
 
     owners = [ids[0, r] // F for r in range(F)]
     rank = []
@@ -78,16 +85,20 @@
             before = before + jnp.where(owners[s] == owners[r], 1, 0)
         rank.append(before)
 
+    line = lax.broadcasted_iota(jnp.int32, (W, C), 0)
+
     def pack(k):
         owner = (z + k) % T
+        targets = jnp.zeros((W, C), F32)
         for s in range(CAP):
             row, target = jnp.int32(0), jnp.int32(-1)
             for r in range(F):
                 hit = jnp.logical_and(owners[r] == owner, rank[r] == s)
                 row = jnp.where(hit, r, row)
                 target = jnp.where(hit, ids[0, r] - owner * F, target)
-            slots[k, s, 0:H] = loaded[row]
-            slots[k, s, H] = jnp.full((W, C), target.astype(F32), F32).astype(BF16)
+            slots[k, s * H : (s + 1) * H] = loaded[row]
+            targets = jnp.where(line == s, target.astype(F32), targets)
+        slots[k, CAP * H] = targets.astype(BF16)
 
     each(0, T, pack)
     pl.semaphore_wait(barrier, 1 + (Q - 1) + (T - 1))
@@ -109,11 +120,12 @@
     if T * U > 3 * R:
         z32[3 * R :] = jnp.zeros((T * U - 3 * R, C), F32)
         z16[3 * R :] = jnp.zeros((T * U - 3 * R, C), BF16)
-    load_w.wait()
+    loads[2].wait()
     for p in range(9):
         for j in range(3):
             wt[p, j * C : (j + 1) * C, :] = w[p, j * C : (j + 1) * C, :].T
-    load_og.wait()
+    loads[3].wait()
+    loads[4].wait()
 
     each(1, T, lambda k: row_copy(k).wait_recv())
 
@@ -122,9 +134,9 @@
         for k in range(T):
             source = slots if k == 0 else rslots
             for s in range(CAP):
-                gap = jnp.abs(source[k, s, H] - jnp.asarray(f, BF16))
-                weight = jnp.maximum(jnp.asarray(1, BF16) - gap, jnp.asarray(0, BF16))
-                picked = picked + source[k, s, 0:H] * weight[None]
+                gap = jnp.abs(source[k, CAP * H, s : s + 1].astype(F32) - f)
+                weight = jnp.broadcast_to(jnp.maximum(1.0 - gap, 0.0), (W, C)).astype(BF16)
+                picked = picked + source[k, s * H : (s + 1) * H] * weight[None]
         frames[f + 2] = picked
 
     for f in (F - 2, F - 1):
@@ -386,6 +398,30 @@
     each(0, T, lambda kz: each(0, Q, lambda k: gather_pair(kz, k).wait_send()))
 
 
+def finish_body(
+    D, R, scale, act, igrad, total, bgrad, act_out, igrad_out, kernel_out, bias_out,
+    kernel_grad, bias_grad, sem,
+):
+    rows = kernel_grad.shape[1]
+    copies = [
+        pltpu.make_async_copy(act, act_out, sem.at[0]),
+        pltpu.make_async_copy(igrad, igrad_out, sem.at[1]),
+        pltpu.make_async_copy(bias_grad, bias_out, sem.at[2]),
+    ]
+    copies[0].start()
+    copies[1].start()
+    bias_grad[...] = bgrad[...] * scale
+    copies[2].start()
+    for a in range(3):
+        for b in range(pl.cdiv(rows, R)):
+            n = min(R, rows - b * R)
+            kernel_grad[a, b * R : b * R + n] = total[b, a * R : a * R + n].astype(F32) * scale
+        copies.append(pltpu.make_async_copy(kernel_grad.at[a], kernel_out.at[a], sem.at[3 + a]))
+        copies[-1].start()
+    for copy in copies:
+        copy.wait()
+
+
 def body(T, D, loaded, frame_index, out_grad, kernel, conv_bias):
     _, F, H, W, C = loaded.shape
     Q = D // 2
@@ -394,7 +430,7 @@
     U = 16 * pl.cdiv(3 * R // 16, T)
     dims = (T, D, F, H, W, C, R, U)
     vmem = pl.BlockSpec(memory_space=pltpu.VMEM)
-    hbm = pl.BlockSpec(memory_space=pl.ANY)
+    hbm = pl.BlockSpec(memory_space=pltpu.HBM)
     V = pltpu.VMEM
     S = pltpu.SemaphoreType.DMA
     act, igrad, total, bgrad = pl.pallas_call(
@@ -405,11 +441,12 @@
             jax.ShapeDtypeStruct((D, T, U, C), BF16),
             jax.ShapeDtypeStruct((1, C), F32),
         ),
-        in_specs=[pl.BlockSpec(memory_space=pltpu.SMEM), vmem, hbm, hbm, vmem],
+        in_specs=[hbm] * 5,
         out_specs=(vmem, vmem, vmem, vmem),
         scratch_shapes=[
+            pltpu.SMEM((1, F), jnp.int32), V((F, H, W, C), BF16), V((1, C), F32),
             V((F, H, W, C), BF16), V((9, K3, C), BF16), V((9, K3, C), BF16),
-            V((T, CAP, H + 1, W, C), BF16), V((T, CAP, H + 1, W, C), BF16),
+            V((T, CAP * H + 1, W, C), BF16), V((T, CAP * H + 1, W, C), BF16),
             V((F + 6, H, W, C), BF16),
             V((F + 2, H + 2, W, K3), BF16), V((K3, (F + 2) * HW), BF16),
             V((F + 2, H + 2, W, K3), BF16),
@@ -418,7 +455,7 @@
             V((3, Q, R, C), BF16), V((T * U, C), F32), V((T * U, C), BF16),
             V((T, U, C), BF16),
             V((8, C), F32), V((8, C), F32), V((Q, 8, C), F32), V((T, 8, C), F32),
-            S((2,)), S((T,)), S((T,)), S, S, S, S,
+            S((5,)), S((T,)), S((T,)), S, S, S, S,
             S((3,)), S((3,)), S((3, Q)), S((3, Q)), S((T,)), S((T,)),
             S((T,)), S((T,)), S((T, Q)), S((T, Q)), S((T, Q)), S((T, Q)),
             S, S, S((Q,)), S((Q,)), S((T,)), S((T,)),
@@ -426,12 +463,25 @@
         compiler_params=pltpu.CompilerParams(
             collective_id=0, has_side_effects=True, vmem_limit_bytes=48 * 1024 * 1024
         ),
-    )(frame_index, loaded[0], out_grad[0], kernel.reshape(9, K3, C), conv_bias[None])
+    )(*(
+        pltpu.with_memory_space_constraint(x, pltpu.HBM)
+        for x in (frame_index, loaded[0], out_grad[0], kernel.reshape(9, K3, C), conv_bias[None])
+    ))
     scale = 1.0 / math.sqrt(T * F * HW * D * loaded.shape[0])
-    rows = total.reshape(D, T * U, C)[:, : 3 * R].reshape(D, 3, R, C)
-    rows = jnp.swapaxes(rows, 0, 1).reshape(3, D * R, C)[:, : 3 * K3]
-    kernel_grad = (rows.astype(F32) * scale).reshape(kernel.shape)
-    return act[None], igrad[None], kernel_grad, bgrad[0] * scale
+    act, igrad, kernel_grad, bias_grad = pl.pallas_call(
+        functools.partial(finish_body, D, R, scale),
+        out_shape=(
+            jax.ShapeDtypeStruct((F, H, W, C), BF16),
+            jax.ShapeDtypeStruct((F, H, W, C), BF16),
+            jax.ShapeDtypeStruct((3, 3 * K3, C), F32),
+            jax.ShapeDtypeStruct((1, C), F32),
+        ),
+        in_specs=[vmem] * 4,
+        out_specs=[hbm] * 4,
+        scratch_shapes=[V((3, 3 * K3, C), F32), V((1, C), F32), S((6,))],
+        compiler_params=pltpu.CompilerParams(vmem_limit_bytes=8 * 1024 * 1024),
+    )(act, igrad, total.reshape(D, T * U, C), bgrad)
+    return act[None], igrad[None], kernel_grad.reshape(kernel.shape), bias_grad[0]
 
 
 def solution(mesh):

time: 53.2 us -> 45.4 us (0.85)
  local copies, waits for them, and re-layouts: 7.11 us -> 0 us
  other arithmetic: 0.65 us -> 0 us
    unnamed x12 -> x0, local copies, waits for them, and re-layouts: 5.77 us -> none
    pallas_call x0 -> x1, Pallas kernels: none -> 1.43 us  [body(): pl.pallas_call(functools.partial(finish_body, D, R, scale), out_shape=(ja...]
    mul x1 -> x0, local copies, waits for them, and re-layouts: 1.34 us -> none  [body(): kernel_grad = (rows.astype(F32) * scale).reshape(kernel.shape)]
    pallas_call x1, Pallas kernels: 44.5 us -> 43.2 us  [body(): pl.pallas_call(functools.partial(kernel_body, dims), out_shape=(jax.Shape...]
    mul x2 -> x0, other arithmetic: 0.65 us -> none  [the longest x1 0.51 us: body(): return (act[None], igrad[None], kernel_grad, bgrad[0] * scale)]
where the time goes in v1:
time: 45.4 us; the launch traced here: 45.3 us
  Pallas kernels  44.6 us (98%)
  between operations  0.64 us (1%)
    pallas_call x1, Pallas kernels, body(): pl.pallas_call(functools.partial(kernel_body, dims), out_shape=(jax.Shape...  43.2 us
    pallas_call x1, Pallas kernels, body(): pl.pallas_call(functools.partial(finish_body, D, R, scale), out_shape=(ja...  1.43 us

profile of v1, /device:TPU:0, one launch (start us, length us, event | category | flops | bytes accessed | tf_op | source)
XLA Modules:
  0.0 45.3 jit_solution(9262828776963951373)
XLA Ops:
  0.6 43.2 %shard_map.84 = (bf16[8,8,16,128]{3,2,1,0:T(8,128)(2,1)S(1)}, bf16[8,8,16,128]{3,2,1,0:T(8,128)(2,1)S(1)}, bf16[8,4,112,128]{3,2,1,0:T(8,128)(2,1)S(1)}, f32[1,128]{1,0:T(1,128)S(1)}) custom-call(s32[1,8]{1,0:T(1,128)} %ids_hbm.1, bf16[8,8,16,128]{3,2,1,0:T(8,128)(2,1)} %bitcast.11, bf16[8,8,16,128]{3,2,1,0:T(8,128)(2,1)} %bitcast.12, ...), custom_call_target="tpu_custom_call" | custom-call | tf_op jit(solution)/shard_map/pallas_call | solution.py:436
  43.8 1.4 %shard_map.85 = (bf16[8,8,16,128]{3,2,1,0:T(8,128)(2,1)}, bf16[8,8,16,128]{3,2,1,0:T(8,128)(2,1)}, f32[3,1152,128]{2,1,0:T(8,128)}, f32[1,128]{1,0:T(1,128)}) custom-call(bf16[8,8,16,128]{3,2,1,0:T(8,128)(2,1)S(1)} %get-tuple-element.12.act, bf16[8,8,16,128]{3,2,1,0:T(8,128)(2,1)S(1)} %get-tuple-element.13.igrad, bf16[8,448,128]{2,1,0:T(8,128)(2,1)S(1)} %bitcast.9, ...), custom_call_target="tpu_custom_call" | custom-call | tf_op jit(solution)/shard_map/pallas_call | solution.py:471

commit v2 on v1

--- a/solution.py
+++ b/solution.py
@@ -28,7 +28,7 @@
     ld_sem, f_s, f_r, h_s, h_r, g_s, g_r, p_s, p_r, x_s, x_r, zs_s, zs_r,
     az_s, az_r, ax_s, ax_r, ap_s, ap_r, bp_s, bp_r, bx_s, bx_r, bz_s, bz_r,
 ):
-    T, D, F, H, W, C, R, U = dims
+    T, D, F, H, W, C, R, U, pieces = dims
     Q = D // 2
     HW = H * W
     K3 = 3 * C
@@ -117,9 +117,10 @@
         for a in range(3):
             dwf[a, taps_rows:] = jnp.zeros((D * R - taps_rows, C), F32)
             dwb[a, taps_rows:] = jnp.zeros((D * R - taps_rows, C), BF16)
-    if T * U > 3 * R:
-        z32[3 * R :] = jnp.zeros((T * U - 3 * R, C), F32)
-        z16[3 * R :] = jnp.zeros((T * U - 3 * R, C), BF16)
+    if pieces * U > R:
+        for a in range(3):
+            z32[a, R:] = jnp.zeros((pieces * U - R, C), F32)
+            z16[a, R:] = jnp.zeros((pieces * U - R, C), BF16)
     loads[2].wait()
     for p in range(9):
         for j in range(3):
@@ -226,9 +227,18 @@
             s16.at[a, there], xy_in.at[a, k], x_s.at[a, k], x_r.at[a, k], to_q(k)
         )
 
-    def z_copy(k):
-        there = pl.ds(pl.multiple_of(((z + k) % T) * U, 16), U)
-        return remote(z16.at[there], z_in.at[k], zs_s.at[k], zs_r.at[k], to_z(k))
+    def duty(a, k):
+        return (z + k + 4 * T - a) % T
+
+    def if_duty(a, k, action):
+        pl.when(duty(a, k) < pieces)(action)
+
+    def piece_rows(a, k):
+        return pl.ds(pl.multiple_of(jnp.minimum(duty(a, k), pieces - 1) * U, 16), U)
+
+    def z_copy(a, k):
+        there = piece_rows(a, k)
+        return remote(z16.at[a, there], z_in.at[a, k], zs_s.at[a, k], zs_r.at[a, k], to_z(k))
 
     def bias_pair():
         return remote(b_own, b_pair, bp_s, bp_r, other)
@@ -290,55 +300,72 @@
                 out = out + jnp.dot(rows, wt[a * 3 + i], preferred_element_type=F32)
         igrad[t : t + n] = out.astype(BF16).reshape(n, H, W, C)
 
-    backward(0, 2)
-    backward(2, 2)
-
     def after_xy(a):
         here = pl.ds(pl.multiple_of(q * R, 16), R)
         each(1, Q, lambda k: xy_copy(a, k).wait_recv())
         got = s32[a, here]
         for k in range(1, Q):
             got = got + xy_in[a, k].astype(F32)
-        z32[a * R : (a + 1) * R] = got
-        z16[a * R : (a + 1) * R] = got.astype(BF16)
-
-    for a in range(3):
-        after_xy(a)
-    each(1, T, lambda k: z_copy(k).start())
+        z32[a, 0:R] = got
+        z16[a, 0:R] = got.astype(BF16)
+        each(1, T, lambda k: if_duty(a, k, lambda: z_copy(a, k).start()))
+
+    def gather_z(a, k):
+        piece = total.at[c * Q + q, a, piece_rows(a, 0)]
+        return remote(piece, piece, az_s.at[a, k], az_r.at[a, k], to_z(k))
+
+    def gather_q(a, kz, k):
+        piece = total.at[c * Q + q, a, piece_rows(a, -kz)]
+        return remote(piece, piece, ax_s.at[a, kz, k], ax_r.at[a, kz, k], to_q(k))
+
+    def gather_pair(a, k):
+        block = total.at[c * Q + (q + Q - k) % Q, a]
+        return remote(block, block, ap_s.at[a, k], ap_r.at[a, k], other)
+
+    def after_z(a):
+        def sum_up():
+            each(1, T, lambda k: z_copy(a, k).wait_recv())
+            got = z32[a, piece_rows(a, 0)]
+            for k in range(1, T):
+                got = got + z_in[a, k].astype(F32)
+            total[c * Q + q, a, piece_rows(a, 0)] = got.astype(BF16)
+            each(1, T, lambda k: gather_z(a, k).start())
+            each(1, Q, lambda k: gather_q(a, 0, k).start())
+
+        if_duty(a, 0, sum_up)
+
+    def relay_z(a):
+        def one(kz):
+            def pass_on():
+                gather_z(a, kz).wait_recv()
+                each(1, Q, lambda k: gather_q(a, kz, k).start())
+
+            if_duty(a, -kz, pass_on)
+
+        each(1, T, one)
+        gather_pair(a, 0).start()
+
+    def relay_q(a):
+        def one(k):
+            each(0, T, lambda kz: if_duty(a, -kz, lambda: gather_q(a, kz, k).wait_recv()))
+            gather_pair(a, k).start()
+
+        each(1, Q, one)
+
+    backward(0, 2)
+    after_xy(0)
+    backward(2, 2)
+    after_xy(1)
+    after_xy(2)
     each(1, Q, lambda k: bias_q(k).wait_recv())
     got = bx[0]
     for k in range(1, Q):
         got = got + bx[k]
     bz[z] = got
     each(1, T, lambda k: bias_z(k).start())
-
     backward(4, 2)
-
-    each(1, T, lambda k: z_copy(k).wait_recv())
-    got = z32[pl.ds(pl.multiple_of(z * U, 16), U)]
-    for k in range(1, T):
-        got = got + z_in[k].astype(F32)
-    block = c * Q + q
-    total[block, z] = got.astype(BF16)
-
-    def piece(k, kz):
-        return total.at[c * Q + (q + Q - k) % Q, (z + T - kz) % T]
-
-    def gather_z(k):
-        return remote(piece(0, 0), piece(0, 0), az_s.at[k], az_r.at[k], to_z(k))
-
-    def gather_q(kz, k):
-        return remote(piece(0, kz), piece(0, kz), ax_s.at[kz, k], ax_r.at[kz, k], to_q(k))
-
-    def gather_pair(kz, k):
-        return remote(piece(k, kz), piece(k, kz), ap_s.at[kz, k], ap_r.at[kz, k], other)
-
-    def send_on(kz):
-        each(1, Q, lambda k: gather_q(kz, k).start())
-        gather_pair(kz, 0).start()
-
-    each(1, T, lambda k: gather_z(k).start())
-    send_on(0)
+    after_z(0)
+    after_z(1)
 
     @pl.when(z < T - 1)
     def _():
@@ -352,21 +379,14 @@
         mid = frames[F + 4 + t]
         gc[F + t, 1 : H + 1, :, C : 2 * C] = mid
         spread_gate(F + t, mid.reshape(HW, C))
-
-    def relay_z(kz):
-        gather_z(kz).wait_recv()
-        send_on(kz)
-
-    def relay_q(kz):
-        def one(k):
-            gather_q(kz, k).wait_recv()
-            gather_pair(kz, k).start()
-
-        each(1, Q, one)
-
-    each(1, T, relay_z)
+    after_z(2)
+    relay_z(0)
     backward(6, 2)
-    each(0, T, relay_q)
+    relay_z(1)
+    relay_q(0)
+    relay_z(2)
+    relay_q(1)
+    relay_q(2)
 
     each(1, T, lambda k: bias_z(k).wait_recv())
     got = bz[0]
@@ -374,7 +394,7 @@
         got = got + bz[k]
     bgrad[...] = jnp.sum(got, axis=0, keepdims=True)
 
-    each(0, T, lambda kz: each(0, Q, lambda k: gather_pair(kz, k).wait_recv()))
+    each(0, 3, lambda a: each(0, Q, lambda k: gather_pair(a, k).wait_recv()))
 
     each(1, T, lambda k: row_copy(k).wait_send())
 
@@ -392,10 +412,22 @@
     for a in range(3):
         pair_copy(a).wait_send()
         each(1, Q, lambda k: xy_copy(a, k).wait_send())
-    each(1, T, lambda k: z_copy(k).wait_send())
-    each(1, T, lambda k: gather_z(k).wait_send())
-    each(0, T, lambda kz: each(1, Q, lambda k: gather_q(kz, k).wait_send()))
-    each(0, T, lambda kz: each(0, Q, lambda k: gather_pair(kz, k).wait_send()))
+    for a in range(3):
+        each(1, T, lambda k: if_duty(a, k, lambda: z_copy(a, k).wait_send()))
+
+        def gathered():
+            each(1, T, lambda k: gather_z(a, k).wait_send())
+
+        if_duty(a, 0, gathered)
+
+        def passed_on(kz):
+            def sent():
+                each(1, Q, lambda k: gather_q(a, kz, k).wait_send())
+
+            if_duty(a, -kz, sent)
+
+        each(0, T, passed_on)
+        each(0, Q, lambda k: gather_pair(a, k).wait_send())
 
 
 def finish_body(
@@ -415,7 +447,7 @@
     for a in range(3):
         for b in range(pl.cdiv(rows, R)):
             n = min(R, rows - b * R)
-            kernel_grad[a, b * R : b * R + n] = total[b, a * R : a * R + n].astype(F32) * scale
+            kernel_grad[a, b * R : b * R + n] = total[b, a, 0:n].astype(F32) * scale
         copies.append(pltpu.make_async_copy(kernel_grad.at[a], kernel_out.at[a], sem.at[3 + a]))
         copies[-1].start()
     for copy in copies:
@@ -427,8 +459,9 @@
     Q = D // 2
     K3, HW = 3 * C, H * W
     R = 16 * pl.cdiv(pl.cdiv(3 * K3, 16), D)
-    U = 16 * pl.cdiv(3 * R // 16, T)
-    dims = (T, D, F, H, W, C, R, U)
+    U = 16 * pl.cdiv(R // 16, T)
+    pieces = pl.cdiv(R, U)
+    dims = (T, D, F, H, W, C, R, U, pieces)
     vmem = pl.BlockSpec(memory_space=pltpu.VMEM)
     hbm = pl.BlockSpec(memory_space=pltpu.HBM)
     V = pltpu.VMEM
@@ -438,7 +471,7 @@
         out_shape=(
             jax.ShapeDtypeStruct((F, H, W, C), BF16),
             jax.ShapeDtypeStruct((F, H, W, C), BF16),
-            jax.ShapeDtypeStruct((D, T, U, C), BF16),
+            jax.ShapeDtypeStruct((D, 3, pieces * U, C), BF16),
             jax.ShapeDtypeStruct((1, C), F32),
         ),
         in_specs=[hbm] * 5,
@@ -452,12 +485,12 @@
             V((F + 2, H + 2, W, K3), BF16),
             V((3, D * R, C), F32), V((3, D * R, C), BF16),
             V((3, Q * R, C), BF16), V((3, Q * R, C), F32), V((3, Q * R, C), BF16),
-            V((3, Q, R, C), BF16), V((T * U, C), F32), V((T * U, C), BF16),
-            V((T, U, C), BF16),
+            V((3, Q, R, C), BF16), V((3, pieces * U, C), F32), V((3, pieces * U, C), BF16),
+            V((3, T, U, C), BF16),
             V((8, C), F32), V((8, C), F32), V((Q, 8, C), F32), V((T, 8, C), F32),
             S((5,)), S((T,)), S((T,)), S, S, S, S,
-            S((3,)), S((3,)), S((3, Q)), S((3, Q)), S((T,)), S((T,)),
-            S((T,)), S((T,)), S((T, Q)), S((T, Q)), S((T, Q)), S((T, Q)),
+            S((3,)), S((3,)), S((3, Q)), S((3, Q)), S((3, T)), S((3, T)),
+            S((3, T)), S((3, T)), S((3, T, Q)), S((3, T, Q)), S((3, Q)), S((3, Q)),
             S, S, S((Q,)), S((Q,)), S((T,)), S((T,)),
         ],
         compiler_params=pltpu.CompilerParams(
@@ -480,7 +513,7 @@
         out_specs=[hbm] * 4,
         scratch_shapes=[V((3, 3 * K3, C), F32), V((1, C), F32), S((6,))],
         compiler_params=pltpu.CompilerParams(vmem_limit_bytes=8 * 1024 * 1024),
-    )(act, igrad, total.reshape(D, T * U, C), bgrad)
+    )(act, igrad, total, bgrad)
     return act[None], igrad[None], kernel_grad.reshape(kernel.shape), bias_grad[0]
 
 

time: 45.4 us -> 44.7 us (0.985)
  Pallas kernels: 44.6 us -> 43.8 us
    pallas_call x1, Pallas kernels: 43.2 us -> 42.4 us  [body(): pl.pallas_call(functools.partial(kernel_body, dims), out_shape=(jax.Shape...]
where the time goes in v2:
time: 44.7 us; the launch traced here: 44.5 us
  Pallas kernels  43.8 us (98%)
  between operations  0.64 us (1%)
    pallas_call x1, Pallas kernels, body(): pl.pallas_call(functools.partial(kernel_body, dims), out_shape=(jax.Shape...  42.4 us
    pallas_call x1, Pallas kernels, body(): pl.pallas_call(functools.partial(finish_body, D, R, scale), out_shape=(ja...  1.43 us

profile of v2, /device:TPU:0, one launch (start us, length us, event | category | flops | bytes accessed | tf_op | source)
XLA Modules:
  0.0 44.5 jit_solution(3937406777183891876)
XLA Ops:
  0.6 42.4 %shard_map.84 = (bf16[8,8,16,128]{3,2,1,0:T(8,128)(2,1)S(1)}, bf16[8,8,16,128]{3,2,1,0:T(8,128)(2,1)S(1)}, bf16[8,3,144,128]{3,2,1,0:T(8,128)(2,1)S(1)}, f32[1,128]{1,0:T(1,128)S(1)}) custom-call(s32[1,8]{1,0:T(1,128)} %ids_hbm.1, bf16[8,8,16,128]{3,2,1,0:T(8,128)(2,1)} %bitcast.9, bf16[8,8,16,128]{3,2,1,0:T(8,128)(2,1)} %bitcast.10, ...), custom_call_target="tpu_custom_call" | custom-call | tf_op jit(solution)/shard_map/pallas_call | solution.py:469
  43.0 1.4 %shard_map.85 = (bf16[8,8,16,128]{3,2,1,0:T(8,128)(2,1)}, bf16[8,8,16,128]{3,2,1,0:T(8,128)(2,1)}, f32[3,1152,128]{2,1,0:T(8,128)}, f32[1,128]{1,0:T(1,128)}) custom-call(bf16[8,8,16,128]{3,2,1,0:T(8,128)(2,1)S(1)} %get-tuple-element.12.act, bf16[8,8,16,128]{3,2,1,0:T(8,128)(2,1)S(1)} %get-tuple-element.13.igrad, ...), custom_call_target="tpu_custom_call" | custom-call | tf_op jit(solution)/shard_map/pallas_call | solution.py:504

commit v3 on v2

--- a/solution.py
+++ b/solution.py
@@ -356,36 +356,36 @@
     after_xy(0)
     backward(2, 2)
     after_xy(1)
+    backward(4, 2)
+    after_z(0)
     after_xy(2)
+
+    @pl.when(z < T - 1)
+    def _():
+        gate_copy().wait_recv()
+
+    @pl.when(z == T - 1)
+    def _():
+        frames[F + 4 : F + 6] = jnp.zeros((2, H, W, C), BF16)
+
+    for t in range(2):
+        mid = frames[F + 4 + t]
+        gc[F + t, 1 : H + 1, :, C : 2 * C] = mid
+        spread_gate(F + t, mid.reshape(HW, C))
+    relay_z(0)
+    after_z(1)
     each(1, Q, lambda k: bias_q(k).wait_recv())
     got = bx[0]
     for k in range(1, Q):
         got = got + bx[k]
     bz[z] = got
     each(1, T, lambda k: bias_z(k).start())
-    backward(4, 2)
-    after_z(0)
-    after_z(1)
-
-    @pl.when(z < T - 1)
-    def _():
-        gate_copy().wait_recv()
-
-    @pl.when(z == T - 1)
-    def _():
-        frames[F + 4 : F + 6] = jnp.zeros((2, H, W, C), BF16)
-
-    for t in range(2):
-        mid = frames[F + 4 + t]
-        gc[F + t, 1 : H + 1, :, C : 2 * C] = mid
-        spread_gate(F + t, mid.reshape(HW, C))
+    backward(6, 2)
+    relay_q(0)
+    relay_z(1)
     after_z(2)
-    relay_z(0)
-    backward(6, 2)
-    relay_z(1)
-    relay_q(0)
+    relay_q(1)
     relay_z(2)
-    relay_q(1)
     relay_q(2)
 
     each(1, T, lambda k: bias_z(k).wait_recv())

time: 44.7 us -> 48.3 us (1.081)
  Pallas kernels: 43.8 us -> 47.5 us
    pallas_call x1, Pallas kernels: 42.4 us -> 46.1 us  [body(): pl.pallas_call(functools.partial(kernel_body, dims), out_shape=(jax.Shape...]
where the time goes in v3:
time: 48.3 us; the launch traced here: 48.1 us
  Pallas kernels  47.5 us (98%)
  between operations  0.64 us (1%)
    pallas_call x1, Pallas kernels, body(): pl.pallas_call(functools.partial(kernel_body, dims), out_shape=(jax.Shape...  46.1 us
    pallas_call x1, Pallas kernels, body(): pl.pallas_call(functools.partial(finish_body, D, R, scale), out_shape=(ja...  1.43 us

profile of v3, /device:TPU:0, one launch (start us, length us, event | category | flops | bytes accessed | tf_op | source)
XLA Modules:
  0.0 48.1 jit_solution(3814032828965127937)
XLA Ops:
  0.6 46.1 %shard_map.84 = (bf16[8,8,16,128]{3,2,1,0:T(8,128)(2,1)S(1)}, bf16[8,8,16,128]{3,2,1,0:T(8,128)(2,1)S(1)}, bf16[8,3,144,128]{3,2,1,0:T(8,128)(2,1)S(1)}, f32[1,128]{1,0:T(1,128)S(1)}) custom-call(s32[1,8]{1,0:T(1,128)} %ids_hbm.1, bf16[8,8,16,128]{3,2,1,0:T(8,128)(2,1)} %bitcast.9, bf16[8,8,16,128]{3,2,1,0:T(8,128)(2,1)} %bitcast.10, ...), custom_call_target="tpu_custom_call" | custom-call | tf_op jit(solution)/shard_map/pallas_call | solution.py:469
  46.7 1.4 %shard_map.85 = (bf16[8,8,16,128]{3,2,1,0:T(8,128)(2,1)}, bf16[8,8,16,128]{3,2,1,0:T(8,128)(2,1)}, f32[3,1152,128]{2,1,0:T(8,128)}, f32[1,128]{1,0:T(1,128)}) custom-call(bf16[8,8,16,128]{3,2,1,0:T(8,128)(2,1)S(1)} %get-tuple-element.12.act, bf16[8,8,16,128]{3,2,1,0:T(8,128)(2,1)S(1)} %get-tuple-element.13.igrad, ...), custom_call_target="tpu_custom_call" | custom-call | tf_op jit(solution)/shard_map/pallas_call | solution.py:504
